TPU v7x, 32 devices: a whole 2x2x4 slice. The times are simulated.
32 devices in a mesh: scen: 2 (over x), row: 4 (over y, core), col: 4 (over z).
Axes of the slice: x: 2, y: 2, z: 4, core: 2. Of those that a mesh axis runs over, the one named last changes fastest.
Arguments:
- root_matrix: float32 [8192, 8192], P(('scen', 'row'), 'col'), may hold values from -1 to 32, as said below
- inverse_block: bfloat16 [32, 1024, 1024], P(('scen', 'row', 'col')), may hold values from -0.05 to 3, as said below
- link_tiles: bfloat16 [32, 20, 1024, 128], P(('scen', 'row', 'col')), may hold values from -0.1875 to 0.1875
- tile_mask: int32 [32, 64], P(('scen', 'row', 'col')), may hold values from 0 to 1, as said below
- panel_index: int32 [1], replicated, may hold values from 0 to 31
Outputs:
- trailing: float32 [8192, 8192], P(('scen', 'row'), 'col')
- factor: float32 [8192, 128], P(('scen', 'row', 'col'))
Inputs may be any that keep to these rules, and one draw needn't show every extreme that they name: `root_matrix`: Symmetric, with the diagonal between 8 and 32 and every other entry of magnitude under 1. `inverse_block`: each block is symmetric positive definite, its diagonal between 1 and 3. `tile_mask`: each scenario flags between 4 and 20 tiles, at most 4 among each aligned group of 8 tiles (tiles 0 to 7, and so on); some scenario flags exactly 20 tiles, 4 in each of its first groups.
All inputs are finite; a program needn't handle non-finite values.
Results may differ from a plain program's by a relative error of at most 0.00049.
Values may be sent and summed in bfloat16 or wider, within the bound.
A program may use at most 64 MiB of HBM per device.

v0:
```python
import jax
import jax.numpy as jnp
from jax import lax
from jax.sharding import PartitionSpec as P

PANEL = 128


def broadcast(block, axis, source):
    block = jnp.where(lax.axis_index(axis) == source, block, jnp.zeros_like(block))
    return lax.psum(block, axis)


def select_matrix(tile_flags, slot_count):
    slot_order = jnp.cumsum(tile_flags) - 1
    slot_ids = lax.broadcasted_iota(jnp.int32, (slot_count, tile_flags.shape[0]), 0)
    hit = (slot_order[None, :] == slot_ids) & (tile_flags[None, :] == 1)
    return jnp.where(hit, jnp.float32(1.0), jnp.float32(0.0))


def compact_term(inverse, tiles_here, tile_flags, panel_at):
    slot_count, inner_rows, tile_rows = tiles_here.shape
    selector = select_matrix(tile_flags, slot_count)
    per_panel = PANEL // tile_rows
    picked = lax.dynamic_slice_in_dim(selector, panel_at * per_panel, per_panel, 1)
    columns = jnp.einsum(
        "kj,knt->njt", picked.astype(jnp.bfloat16), tiles_here, preferred_element_type=jnp.float32
    )
    columns = columns.reshape(inner_rows, PANEL).astype(jnp.bfloat16)
    weighted = jnp.dot(inverse, columns, preferred_element_type=jnp.float32).astype(jnp.bfloat16)
    product = jnp.einsum("knt,na->kta", tiles_here, weighted, preferred_element_type=jnp.float32)
    return (selector, product)


def dense_term(selector, product, base_cols, base_start):
    spread = jnp.einsum("kr,kta->rta", selector, product, precision=lax.Precision.HIGHEST)
    scenario = spread.reshape(selector.shape[1] * product.shape[1], PANEL)
    own_block = lax.dynamic_slice_in_dim(scenario, base_start, base_cols.shape[0], 0) + base_cols
    return lax.dynamic_update_slice_in_dim(scenario, own_block, base_start, 0)


def lower_rows(diagonal, rows_here, first_row, first_col):
    chol_lower = jnp.linalg.cholesky(diagonal)
    solved = jax.scipy.linalg.solve_triangular(chol_lower, rows_here.T, lower=True).T
    row_ids = first_row + lax.broadcasted_iota(jnp.int32, (rows_here.shape[0], 1), 0)
    return jnp.where(row_ids >= first_col, solved, 0.0)


def trailing_rows(factor_part, first_row, first_col):
    rounded = factor_part.astype(jnp.bfloat16)
    row_ids = first_row + lax.broadcasted_iota(jnp.int32, (factor_part.shape[0], 1), 0)
    return jnp.where(row_ids >= first_col + PANEL, rounded, jnp.zeros_like(rounded))


def local(root_matrix, inverse_block, link_tiles, tile_mask, panel_index):
    panel_at = panel_index[0]
    tile_flags = tile_mask[0]
    selector, product = compact_term(inverse_block[0], link_tiles[0], tile_flags, panel_at)
    tile_count = selector.shape[1]
    tile_rows = product.shape[1]
    total_rows = tile_count * tile_rows
    row_block, col_block = root_matrix.shape
    scen_at = lax.axis_index("scen")
    row_at = lax.axis_index("row")
    col_at = lax.axis_index("col")
    row_count = lax.axis_size("row")
    col_count = lax.axis_size("col")
    scen_count = lax.axis_size("scen")
    block_at = scen_at * row_count + row_at
    first_col = panel_at * PANEL
    owner_col = first_col // col_block
    base_cols = lax.dynamic_slice_in_dim(root_matrix, first_col - owner_col * col_block, PANEL, 1)
    base_cols = jnp.where(col_at == owner_col, base_cols, 0.0)
    piece_rows = row_block // col_count
    scenario = dense_term(selector, product, base_cols, block_at * row_block)
    slab_rows = total_rows // scen_count
    slab_sum = lax.psum_scatter(scenario, "scen", scatter_dimension=0, tiled=True)
    slab_sum = lax.psum(slab_sum, ("row", "col"))
    owner_slab = first_col // slab_rows
    diag_part = lax.dynamic_slice_in_dim(slab_sum, first_col - owner_slab * slab_rows, PANEL, 0)
    diagonal = broadcast(diag_part, "scen", owner_slab)
    slab_first = scen_at * slab_rows
    slab_factor = lower_rows(diagonal, slab_sum, slab_first, first_col)
    factor_rows = lax.dynamic_slice_in_dim(
        slab_factor, (row_at * col_count + col_at) * piece_rows, piece_rows, 0
    )
    ending = trailing_rows(slab_factor, slab_first, first_col)
    all_factor = lax.all_gather(ending, "scen", axis=0, tiled=True)
    own_rows = lax.dynamic_slice_in_dim(all_factor, block_at * row_block, row_block, 0)
    own_cols = lax.dynamic_slice_in_dim(all_factor, col_at * col_block, col_block, 0)
    update = lax.dot_general(
        own_rows, own_cols, (((1,), (1,)), ((), ())), preferred_element_type=jnp.float32
    )
    return (root_matrix - update, factor_rows)


def solution(mesh):
    in_specs = (
        P(("scen", "row"), "col"),
        P(("scen", "row", "col"), None, None),
        P(("scen", "row", "col"), None, None, None),
        P(("scen", "row", "col"), None),
        P(),
    )
    out_specs = (P(("scen", "row"), "col"), P(("scen", "row", "col"), None))
    return jax.shard_map(local, mesh=mesh, in_specs=in_specs, out_specs=out_specs, check_vma=False)
```

profile of v0, /device:TPU:0, one launch (start us, length us, event | category | flops | bytes accessed | tf_op | source)
XLA Modules:
  0.0 295.9 jit_solution(16068640463012025839)
XLA Ops:
  7.2 0.0 copy-start
  7.2 0.0 reduce-scatter.2.cloned.1.call-start
  8.1 0.7 compare_bitcast_fusion
  8.7 0.7 copy.11
  9.5 0.1 reduce-window.8
  9.6 0.1 add_reduce_fusion
  9.7 0.1 fusion.24
  9.8 7.5 %fusion = f32[1,1024,128]{2,0,1:T(1,128)} fusion(bf16[20,1024,128]{2,1,0:T(8,128)(2,1)} %bitcast.50, bf16[20,64]{0,1:T(8,128)(2,1)S(1)} %fusion.24, s32[]{:T(128)S(6)} %select_n.61), kind=kOutput, calls=%fused_computation | convolution fusion | flops 5242880 | bytes 5767684 | tf_op jit(solution)/shard_map/kj,knt->njt/dot_general | solution.py:26
  17.2 0.0 copy-done
  17.3 4.2 %fusion.13 = f32[128,20,128]{2,0,1:T(8,128)S(1)} fusion(bf16[1,1024,1024]{2,1,0:T(8,128)(2,1)S(1)} %copy-done, f32[1024,128]{1,0:T(8,128)} %bitcast.52, bf16[1,20,1024,128]{3,2,1,0:T(8,128)(2,1)} %param.7), kind=kOutput, calls=%fused_computation.11 | convolution fusion | flops 939786240 | bytes 9175040 | tf_op jit(solution)/shard_map/knt,na->kta/dot_general | solution.py:31
  21.4 1.6 copy.17
  23.1 4.9 %fusion.4 = f32[64,128,128]{2,0,1:T(8,128)S(1)} fusion(f32[128,20,128]{0,1,2:T(8,128)} %copy.17, s32[64]{0:T(128)S(1)} %add_reduce_fusion, pred[64]{0:T(512)(128)(4,1)S(1)} %compare_bitcast_fusion), kind=kOutput, calls=%fused_computation.6 | convolution fusion | flops 251662080 | bytes 5505344 | tf_op jit(solution)/shard_map/kr,kta->rta/dot_general | solution.py:36
  27.9 4.4 %copy.13 = f32[64,128,128]{2,1,0:T(8,128)} copy(f32[64,128,128]{2,0,1:T(8,128)S(1)} %fusion.4) | data formatting | bytes 8388608 | tf_op jit(solution)/shard_map/kr,kta->rta/dot_general | solution.py:36
  32.4 2.0 add_dynamic-update-slice_fusion
  34.4 0.0 reduce-scatter.2.cloned.1.call-update
  34.5 0.0 all-reduce.3.cloned.1.call-start
  34.5 57.1 %reduce-scatter.2.cloned.1.call-done = f32[4096,128]{1,0:T(8,128)} async-done(((f32[8192,128]{1,0:T(8,128)}), f32[4096,128]{1,0:T(8,128)}) %reduce-scatter.2.cloned.1.call-update) | async-done | bytes 2097168 | tf_op jit(solution)/shard_map/reduce_scatter | solution.py:77
  91.6 0.0 all-reduce.3.cloned.1.call-update
  91.6 0.0 all-reduce.5.cloned.1.call-start
  91.7 101.6 %all-reduce.3.cloned.1.call-done = f32[4096,128]{1,0:T(8,128)} async-done(((f32[4096,128]{1,0:T(8,128)}), f32[4096,128]{1,0:T(8,128)}) %all-reduce.3.cloned.1.call-update) | async-done | bytes 2097168 | tf_op jit(solution)/shard_map/psum | solution.py:78
  193.4 1.5 dynamic-slice_select_fusion
  194.9 0.0 all-reduce.5.cloned.1.call-update
  194.9 0.2 all-gather.2.cloned.1.call-start
  195.1 21.1 %all-reduce.5.cloned.1.call-done = f32[128,128]{1,0:T(8,128)} async-done(((f32[128,128]{1,0:T(8,128)}), f32[128,128]{1,0:T(8,128)}) %all-reduce.5.cloned.1.call-update) | async-done | bytes 65552 | tf_op jit(solution)/shard_map/psum | solution.py:11
  216.3 0.9 copy.14
  217.2 0.9 fusion.21
  218.0 11.7 %cholesky.15 = f32[128,128]{1,0:T(8,128)S(1)} custom-call(f32[128,128]{1,0:T(8,128)S(1)} %fusion.21), custom_call_target="Cholesky" | custom-call | tf_op jit(solution)/shard_map/jit(cholesky)/cholesky | solution.py:43
  229.8 0.6 compare_reduce_fusion
  230.4 0.7 fusion.19
  231.1 9.8 %custom-call.7 = f32[1,128,128]{1,2,0:T(8,128)S(1)} custom-call(f32[1,128,128]{2,1,0:T(8,128)S(1)} %fusion.19), custom_call_target="InvertDiagBlocksLowerTriangular" | custom-call | tf_op jit(solution)/shard_map/jit(_solve_triangular)/triangular_solve | solution.py:44
  240.9 6.8 %convert_select_fusion = (bf16[4096,128]{1,0:T(8,128)(2,1)}, f32[4096,128]{1,0:T(8,128)}) fusion(pred[4096]{0:T(1024)(128)(4,1)S(1)} %fusion.26, f32[4096,128]{1,0:T(8,128)} %all-reduce.3.cloned.1.call-done, f32[1,128,128]{1,2,0:T(8,128)S(1)} %custom-call.7, pred[4096]{0:T(1024)(128)(4,1)S(1)} %fusion.25), kind=kOutput, calls=%fused_computation.10 | convolution fusion | flops 806879232 | bytes 5316608 | tf_op jit(solution)/shard_map/jit(_solve_triangular)/triangular_solve | solution.py:44
  247.7 0.0 all-gather.2.cloned.1.call-update
  247.8 1.6 constant_dynamic-slice_fusion
  249.3 31.7 %all-gather.2.cloned.1.call-done = bf16[8192,128]{1,0:T(8,128)(2,1)} async-done(((bf16[4096,128]{1,0:T(8,128)(2,1)}), bf16[8192,128]{1,0:T(8,128)(2,1)}) %all-gather.2.cloned.1.call-update) | async-done | bytes 2097168 | tf_op jit(solution)/shard_map/all_gather | solution.py:88
  281.0 8.3 %convolution_subtract_fusion = f32[1024,2048]{1,0:T(8,128)} fusion(f32[1024,2048]{1,0:T(8,128)} %param.5, bf16[8192,128]{1,0:T(8,128)(2,1)} %all-gather.2.cloned.1.call-done, s32[]{:T(128)S(6)} %select_n.74, s32[]{:T(128)S(6)} %select_n.62), kind=kOutput, calls=%fused_computation.3 | convolution fusion | flops 538968064 | bytes 17563656 | tf_op jit(solution)/shard_map/dot_general | solution.py:91
  (3 shorter events, 0.1 us)
Async XLA Ops:
  7.2 10.1 %copy-start = (bf16[1,1024,1024]{2,1,0:T(8,128)(2,1)S(1)}, bf16[1,1024,1024]{2,1,0:T(8,128)(2,1)}, u32[]{:S(2)}) copy-start(bf16[1,1024,1024]{2,1,0:T(8,128)(2,1)} %param.6) | copy-start | bytes 6291460
  7.2 84.4 %reduce-scatter.2.cloned.1.call-start = ((), (), s32[]{:S(2)}) async-start(), calls=%async_computation.1 | async-start | bytes 6291456 | tf_op jit(solution)/shard_map/reduce_scatter | solution.py:77
  34.5 158.9 %all-reduce.3.cloned.1.call-start = ((), (), s32[]{:S(2)}) async-start(), calls=%async_computation.2 | async-start | bytes 4194304 | tf_op jit(solution)/shard_map/psum | solution.py:78
  91.6 124.6 %all-reduce.5.cloned.1.call-start = ((), (), s32[]{:S(2)}) async-start(), calls=%async_computation.3 | async-start | bytes 131072 | tf_op jit(solution)/shard_map/psum | solution.py:11
  194.9 86.2 %all-gather.2.cloned.1.call-start = ((), (), s32[]{:S(2)}) async-start(), calls=%async_computation.4 | async-start | bytes 3145728 | tf_op jit(solution)/shard_map/all_gather | solution.py:88
Sparse Core Ops, SparseCore 0:
  34.6 56.9 reduce-scatter.1
  95.6 97.7 all-reduce.2
  196.2 20.0 all-reduce.4
  247.9 33.1 all-gather.1
where the time goes:
time: 296 us
  waiting for transfers between devices  212 us (72%)
  matrix products  31.7 us (11%)
  other arithmetic  28.2 us (10%)
  between operations  14.7 us (5%)
  local copies, waits for them, and re-layouts  9.31 us (3%)
    psum x1, waiting for transfers between devices, local(): slab_sum = lax.psum(slab_sum, ('row', 'col'))  102 us
    reduce_scatter x1, waiting for transfers between devices, local(): lax.psum_scatter(scenario, 'scen', scatter_dimension=0, tiled=True)  57.1 us
    all_gather x1, waiting for transfers between devices, local(): all_factor = lax.all_gather(ending, 'scen', axis=0, tiled=True)  31.7 us
    psum x1, waiting for transfers between devices, broadcast(): return lax.psum(block, axis)  21.1 us
    another operation x3, other arithmetic, lower_rows(): chol_lower = jnp.linalg.cholesky(diagonal)  12.4 us
    another operation x2, other arithmetic, lower_rows(): jax.scipy.linalg.solve_triangular(chol_lower, rows_here.T, lower=True)  10.5 us
    dot_general x1, matrix products, local(): lax.dot_general(own_rows, own_cols, (((1,), (1,)), ((), ())), preferred_e...  8.3 us
    dot_general x1, matrix products, compact_term(): jnp.einsum('kj,knt->njt', picked.astype(jnp.bfloat16), tiles_here, prefer...  7.47 us
  transfers between devices with their start and end apart: 4, of which 4 were waited for; matrix products, arithmetic and copies ran while one was open for 1% of the time, Pallas kernels for 0%

commit v1 on v0

--- a/solution.py
+++ b/solution.py
@@ -75,7 +75,7 @@
     scenario = dense_term(selector, product, base_cols, block_at * row_block)
     slab_rows = total_rows // scen_count
     slab_sum = lax.psum_scatter(scenario, "scen", scatter_dimension=0, tiled=True)
-    slab_sum = lax.psum(slab_sum, ("row", "col"))
+    slab_sum = lax.psum(lax.psum(slab_sum, "col"), "row")
     owner_slab = first_col // slab_rows
     diag_part = lax.dynamic_slice_in_dim(slab_sum, first_col - owner_slab * slab_rows, PANEL, 0)
     diagonal = broadcast(diag_part, "scen", owner_slab)

time: 296 us -> 337 us (1.14)
  waiting for transfers between devices: 212 us -> 252 us
    psum x1 -> x2, waiting for transfers between devices: 102 us -> 142 us  [local(): slab_sum = lax.psum(lax.psum(slab_sum, 'col'), 'row')]
  transfers between devices with their start and end apart: 4 -> 5, of which waited for: 4 -> 5; matrix products, arithmetic and copies ran while one was open for 1% -> 0% of each run, Pallas kernels for 0% -> 0%
where the time goes in v1:
time: 337 us
  waiting for transfers between devices  252 us (75%)
  matrix products  31.7 us (9%)
  other arithmetic  28.2 us (8%)
  between operations  14.7 us (4%)
  local copies, waits for them, and re-layouts  9.31 us (3%)
    psum x2, waiting for transfers between devices, local(): slab_sum = lax.psum(lax.psum(slab_sum, 'col'), 'row')  142 us
    reduce_scatter x1, waiting for transfers between devices, local(): lax.psum_scatter(scenario, 'scen', scatter_dimension=0, tiled=True)  57.1 us
    all_gather x1, waiting for transfers between devices, local(): all_factor = lax.all_gather(ending, 'scen', axis=0, tiled=True)  31.7 us
    psum x1, waiting for transfers between devices, broadcast(): return lax.psum(block, axis)  21.9 us
    another operation x3, other arithmetic, lower_rows(): chol_lower = jnp.linalg.cholesky(diagonal)  12.4 us
    another operation x2, other arithmetic, lower_rows(): jax.scipy.linalg.solve_triangular(chol_lower, rows_here.T, lower=True)  10.5 us
    dot_general x1, matrix products, local(): lax.dot_general(own_rows, own_cols, (((1,), (1,)), ((), ())), preferred_e...  8.3 us
    dot_general x1, matrix products, compact_term(): jnp.einsum('kj,knt->njt', picked.astype(jnp.bfloat16), tiles_here, prefer...  7.47 us
  transfers between devices with their start and end apart: 5, of which 5 were waited for; matrix products, arithmetic and copies ran while one was open for 0% of the time, Pallas kernels for 0%

profile of v1, /device:TPU:0, one launch (start us, length us, event | category | flops | bytes accessed | tf_op | source)
XLA Modules:
  0.0 336.6 jit_solution(2640348039849032946)
XLA Ops:
  7.2 0.0 copy-start
  7.2 0.0 reduce-scatter.2.cloned.1.call-start
  8.1 0.7 compare_bitcast_fusion
  8.7 0.7 copy.11
  9.5 0.1 reduce-window.8
  9.6 0.1 add_reduce_fusion
  9.7 0.1 fusion.24
  9.8 7.5 %fusion = f32[1,1024,128]{2,0,1:T(1,128)} fusion(bf16[20,1024,128]{2,1,0:T(8,128)(2,1)} %bitcast.50, bf16[20,64]{0,1:T(8,128)(2,1)S(1)} %fusion.24, s32[]{:T(128)S(6)} %select_n.61), kind=kOutput, calls=%fused_computation | convolution fusion | flops 5242880 | bytes 5767684 | tf_op jit(solution)/shard_map/kj,knt->njt/dot_general | solution.py:26
  17.2 0.0 copy-done
  17.3 4.2 %fusion.13 = f32[128,20,128]{2,0,1:T(8,128)S(1)} fusion(bf16[1,1024,1024]{2,1,0:T(8,128)(2,1)S(1)} %copy-done, f32[1024,128]{1,0:T(8,128)} %bitcast.52, bf16[1,20,1024,128]{3,2,1,0:T(8,128)(2,1)} %param.7), kind=kOutput, calls=%fused_computation.11 | convolution fusion | flops 939786240 | bytes 9175040 | tf_op jit(solution)/shard_map/knt,na->kta/dot_general | solution.py:31
  21.4 1.6 copy.17
  23.1 4.9 %fusion.4 = f32[64,128,128]{2,0,1:T(8,128)S(1)} fusion(f32[128,20,128]{0,1,2:T(8,128)} %copy.17, s32[64]{0:T(128)S(1)} %add_reduce_fusion, pred[64]{0:T(512)(128)(4,1)S(1)} %compare_bitcast_fusion), kind=kOutput, calls=%fused_computation.6 | convolution fusion | flops 251662080 | bytes 5505344 | tf_op jit(solution)/shard_map/kr,kta->rta/dot_general | solution.py:36
  27.9 4.4 %copy.13 = f32[64,128,128]{2,1,0:T(8,128)} copy(f32[64,128,128]{2,0,1:T(8,128)S(1)} %fusion.4) | data formatting | bytes 8388608 | tf_op jit(solution)/shard_map/kr,kta->rta/dot_general | solution.py:36
  32.4 2.0 add_dynamic-update-slice_fusion
  34.4 0.0 reduce-scatter.2.cloned.1.call-update
  34.5 0.0 all-reduce.4.cloned.1.call-start
  34.5 57.1 %reduce-scatter.2.cloned.1.call-done = f32[4096,128]{1,0:T(8,128)} async-done(((f32[8192,128]{1,0:T(8,128)}), f32[4096,128]{1,0:T(8,128)}) %reduce-scatter.2.cloned.1.call-update) | async-done | bytes 2097168 | tf_op jit(solution)/shard_map/reduce_scatter | solution.py:77
  91.6 0.0 all-reduce.4.cloned.1.call-update
  91.6 0.0 all-reduce.6.cloned.1.call-start
  91.7 88.9 %all-reduce.4.cloned.1.call-done = f32[4096,128]{1,0:T(8,128)} async-done(((f32[4096,128]{1,0:T(8,128)}), f32[4096,128]{1,0:T(8,128)}) %all-reduce.4.cloned.1.call-update) | async-done | bytes 2097168 | tf_op jit(solution)/shard_map/psum | solution.py:78
  180.6 0.0 all-reduce.6.cloned.1.call-update
  180.7 0.0 all-reduce.8.cloned.1.call-start
  180.8 52.6 %all-reduce.6.cloned.1.call-done = f32[4096,128]{1,0:T(8,128)} async-done(((f32[4096,128]{1,0:T(8,128)}), f32[4096,128]{1,0:T(8,128)}) %all-reduce.6.cloned.1.call-update) | async-done | bytes 2097168 | tf_op jit(solution)/shard_map/psum | solution.py:78
  233.4 1.5 dynamic-slice_select_fusion
  234.8 0.0 all-reduce.8.cloned.1.call-update
  234.9 0.2 all-gather.2.cloned.1.call-start
  235.1 21.9 %all-reduce.8.cloned.1.call-done = f32[128,128]{1,0:T(8,128)} async-done(((f32[128,128]{1,0:T(8,128)}), f32[128,128]{1,0:T(8,128)}) %all-reduce.8.cloned.1.call-update) | async-done | bytes 65552 | tf_op jit(solution)/shard_map/psum | solution.py:11
  257.0 0.9 copy.14
  257.9 0.9 fusion.21
  258.8 11.7 %cholesky.15 = f32[128,128]{1,0:T(8,128)S(1)} custom-call(f32[128,128]{1,0:T(8,128)S(1)} %fusion.21), custom_call_target="Cholesky" | custom-call | tf_op jit(solution)/shard_map/jit(cholesky)/cholesky | solution.py:43
  270.5 0.6 compare_reduce_fusion
  271.2 0.7 fusion.19
  271.9 9.8 %custom-call.7 = f32[1,128,128]{1,2,0:T(8,128)S(1)} custom-call(f32[1,128,128]{2,1,0:T(8,128)S(1)} %fusion.19), custom_call_target="InvertDiagBlocksLowerTriangular" | custom-call | tf_op jit(solution)/shard_map/jit(_solve_triangular)/triangular_solve | solution.py:44
  281.7 6.8 %convert_select_fusion = (bf16[4096,128]{1,0:T(8,128)(2,1)}, f32[4096,128]{1,0:T(8,128)}) fusion(pred[4096]{0:T(1024)(128)(4,1)S(1)} %fusion.26, f32[4096,128]{1,0:T(8,128)} %all-reduce.6.cloned.1.call-done, f32[1,128,128]{1,2,0:T(8,128)S(1)} %custom-call.7, pred[4096]{0:T(1024)(128)(4,1)S(1)} %fusion.25), kind=kOutput, calls=%fused_computation.10 | convolution fusion | flops 806879232 | bytes 5316608 | tf_op jit(solution)/shard_map/jit(_solve_triangular)/triangular_solve | solution.py:44
  288.5 0.0 all-gather.2.cloned.1.call-update
  288.5 1.6 constant_dynamic-slice_fusion
  290.1 31.7 %all-gather.2.cloned.1.call-done = bf16[8192,128]{1,0:T(8,128)(2,1)} async-done(((bf16[4096,128]{1,0:T(8,128)(2,1)}), bf16[8192,128]{1,0:T(8,128)(2,1)}) %all-gather.2.cloned.1.call-update) | async-done | bytes 2097168 | tf_op jit(solution)/shard_map/all_gather | solution.py:88
  321.8 8.3 %convolution_subtract_fusion = f32[1024,2048]{1,0:T(8,128)} fusion(f32[1024,2048]{1,0:T(8,128)} %param.5, bf16[8192,128]{1,0:T(8,128)(2,1)} %all-gather.2.cloned.1.call-done, s32[]{:T(128)S(6)} %select_n.74, s32[]{:T(128)S(6)} %select_n.62), kind=kOutput, calls=%fused_computation.3 | convolution fusion | flops 538968064 | bytes 17563656 | tf_op jit(solution)/shard_map/dot_general | solution.py:91
  (3 shorter events, 0.1 us)
Async XLA Ops:
  7.2 10.1 %copy-start = (bf16[1,1024,1024]{2,1,0:T(8,128)(2,1)S(1)}, bf16[1,1024,1024]{2,1,0:T(8,128)(2,1)}, u32[]{:S(2)}) copy-start(bf16[1,1024,1024]{2,1,0:T(8,128)(2,1)} %param.6) | copy-start | bytes 6291460
  7.2 84.4 %reduce-scatter.2.cloned.1.call-start = ((), (), s32[]{:S(2)}) async-start(), calls=%async_computation.1 | async-start | bytes 6291456 | tf_op jit(solution)/shard_map/reduce_scatter | solution.py:77
  34.5 146.2 %all-reduce.4.cloned.1.call-start = ((), (), s32[]{:S(2)}) async-start(), calls=%async_computation.2 | async-start | bytes 4194304 | tf_op jit(solution)/shard_map/psum | solution.py:78
  91.6 141.7 %all-reduce.6.cloned.1.call-start = ((), (), s32[]{:S(2)}) async-start(), calls=%async_computation.3 | async-start | bytes 4194304 | tf_op jit(solution)/shard_map/psum | solution.py:78
  180.7 76.3 %all-reduce.8.cloned.1.call-start = ((), (), s32[]{:S(2)}) async-start(), calls=%async_computation.4 | async-start | bytes 131072 | tf_op jit(solution)/shard_map/psum | solution.py:11
  234.9 86.9 %all-gather.2.cloned.1.call-start = ((), (), s32[]{:S(2)}) async-start(), calls=%async_computation.5 | async-start | bytes 3145728 | tf_op jit(solution)/shard_map/all_gather | solution.py:88
Sparse Core Ops, SparseCore 0:
  34.6 56.9 reduce-scatter.1
  94.1 86.4 all-reduce.3
  183.0 50.3 all-reduce.5
  236.1 20.8 all-reduce.7
  288.6 33.1 all-gather.1
